TPU v7x, 32 devices: a whole 2x2x4 slice. The times are simulated.
32 devices in a mesh: dp: 8 (over y, x, core), mp: 4 (over z).
Axes of the slice: x: 2, y: 2, z: 4, core: 2. Of those that a mesh axis runs over, the one named last changes fastest.
Arguments:
- tokens: bfloat16 [2048, 8192], P('dp', 'mp'), may hold values from -8 to 8
- attn_gain: bfloat16 [8192], replicated, may hold values from 0.5 to 1.5
- w_query: bfloat16 [8192, 4096], P('dp', 'mp'), may hold values from -2 to 2
- key_projection_weight: bfloat16 [8192, 512], P('dp', 'mp'), may hold values from -2 to 2
- value_projection_weight: bfloat16 [8192, 512], P('dp', 'mp'), may hold values from -0.0625 to 0.0625
- w_out: bfloat16 [4096, 8192], P('mp', 'dp'), may hold values from -0.09375 to 0.09375
- final_gain: bfloat16 [8192], P('mp'), may hold values from 0.5 to 1.5
- unembed: bfloat16 [64128, 8192], P('dp', 'mp'), may hold values from -0.29882812 to 0.29882812
- clean_ids: int32 [8], replicated, may hold values from 0 to 64127, as said below
- corrupt_ids: int32 [8], replicated, may hold values from 0 to 64127
Outputs:
- head_out: bfloat16 [2048, 4096], P('dp', 'mp')
- scores: float32 [8, 32], P('dp', 'mp')
- metric: float32 [8], P('dp')
Inputs may be any that keep to these rules, and one draw needn't show every extreme that they name: `clean_ids`: split the ids into 8 aligned blocks of equal size and number the groups of 1 sequence alike; the block of a clean answer, minus the number of its sequence's group, taken modulo the number of blocks, is drawn so that every such offset occurs for some sequence.
All inputs are finite; a program needn't handle non-finite values.
Results may differ from a plain program's by a relative error of at most 0.015.
Values may be sent and summed in bfloat16 or wider, within the bound.
A program may use at most 128 MiB of HBM per device.

v0:
```python
import math

import jax
import jax.numpy as jnp
from jax import lax
from jax.sharding import PartitionSpec as P

MODEL_WIDTH = 8192
HEAD_SIZE = 128
SEQUENCE_LENGTH = 256


def apply_rotary(tensor, length):
    half_dim = tensor.shape[-1] // 2
    positions = jnp.arange(length, dtype=jnp.float32)
    inv_freq = jnp.exp(
        jnp.arange(half_dim, dtype=jnp.float32) * (-2.0 * math.log(500000.0) / tensor.shape[-1])
    )
    angles = positions[:, None] * inv_freq[None, :]
    cosine_table = jnp.cos(angles)[:, None, :]
    sine_table = jnp.sin(angles)[:, None, :]
    lower_half = tensor[..., :half_dim]
    upper_half = tensor[..., half_dim:]
    return jnp.concatenate(
        [
            lower_half * cosine_table - upper_half * sine_table,
            upper_half * cosine_table + lower_half * sine_table,
        ],
        axis=-1,
    )


def per_device(
    tokens,
    attn_gain,
    w_query,
    key_projection_weight,
    value_projection_weight,
    w_out,
    final_gain,
    unembed,
    clean_ids,
    corrupt_ids,
):
    row_count = tokens.shape[0]
    seq_count = row_count // SEQUENCE_LENGTH
    gathered = lax.all_gather(tokens, "mp", axis=1, tiled=True)
    wide = gathered.astype(jnp.float32)
    normalized_rows = (
        wide
        * lax.rsqrt(jnp.mean(wide * wide, axis=1, keepdims=True) + 1e-05)
        * attn_gain.astype(jnp.float32)
    ).astype(jnp.bfloat16)
    weight_pieces = (
        lax.all_gather(w_query, "dp", axis=0, tiled=True),
        lax.all_gather(key_projection_weight, "dp", axis=0, tiled=True),
        lax.all_gather(value_projection_weight, "dp", axis=0, tiled=True),
    )
    query_raw, key_raw, value_raw = tuple(
        (
            jnp.dot(normalized_rows, weight_piece, preferred_element_type=jnp.float32)
            for weight_piece in weight_pieces
        )
    )
    q_heads = query_raw.shape[1] // HEAD_SIZE
    kv_heads = key_raw.shape[1] // HEAD_SIZE
    query_group_width = q_heads // kv_heads
    queries = apply_rotary(
        query_raw.reshape(seq_count, SEQUENCE_LENGTH, q_heads, HEAD_SIZE), SEQUENCE_LENGTH
    ).astype(jnp.bfloat16)
    projected_key_rows = apply_rotary(
        key_raw.reshape(seq_count, SEQUENCE_LENGTH, kv_heads, HEAD_SIZE), SEQUENCE_LENGTH
    ).astype(jnp.bfloat16)
    value_rows = value_raw.astype(jnp.bfloat16).reshape(
        seq_count, SEQUENCE_LENGTH, kv_heads, HEAD_SIZE
    )
    grouped = queries.reshape(seq_count, SEQUENCE_LENGTH, kv_heads, query_group_width, HEAD_SIZE)
    logits = jnp.einsum(
        "btkgd,bskd->bkgts", grouped, projected_key_rows, preferred_element_type=jnp.float32
    ) / math.sqrt(HEAD_SIZE)
    causal = jnp.arange(SEQUENCE_LENGTH)[:, None] >= jnp.arange(SEQUENCE_LENGTH)[None, :]
    logits = jnp.where(causal, logits, -1e30)
    row_top = jnp.max(logits, axis=-1, keepdims=True)
    exponent = jnp.exp(logits - row_top)
    attn_probs = (exponent / jnp.sum(exponent, axis=-1, keepdims=True)).astype(jnp.bfloat16)
    mixed_heads = jnp.einsum(
        "bkgts,bskd->btkgd", attn_probs, value_rows, preferred_element_type=jnp.float32
    )
    head_out = mixed_heads.astype(jnp.bfloat16).reshape(row_count, q_heads * HEAD_SIZE)
    totals = jnp.sum(head_out.astype(jnp.float32), axis=0)
    all_totals = lax.psum(totals, "dp")
    head_mean = all_totals / (row_count * lax.axis_size("dp"))
    last_out = head_out.reshape(seq_count, SEQUENCE_LENGTH, q_heads * HEAD_SIZE)[
        :, SEQUENCE_LENGTH - 1, :
    ]
    every_last = lax.all_gather(last_out, "dp", axis=0, tiled=True)
    partial_out = jnp.dot(every_last, w_out, preferred_element_type=jnp.float32)
    summed_out = lax.psum(partial_out.astype(jnp.bfloat16), "mp")
    moved_out = lax.all_to_all(summed_out, "dp", split_axis=0, concat_axis=1, tiled=True)
    span = moved_out.shape[1] // lax.axis_size("mp")
    attn_last = lax.dynamic_slice_in_dim(moved_out, lax.axis_index("mp") * span, span, 1)
    last_tokens = tokens.reshape(seq_count, SEQUENCE_LENGTH, tokens.shape[1])[
        :, SEQUENCE_LENGTH - 1, :
    ].astype(jnp.float32)
    residual = last_tokens + attn_last.astype(jnp.float32)
    vocab_rows = unembed.shape[0]
    id_range = lax.axis_index("dp") * vocab_rows + jnp.arange(vocab_rows, dtype=jnp.int32)
    one_hot = (clean_ids[:, None] == id_range[None, :]).astype(jnp.float32) - (
        corrupt_ids[:, None] == id_range[None, :]
    ).astype(jnp.float32)
    direction = lax.psum_scatter(
        jnp.dot(one_hot.astype(jnp.bfloat16), unembed, preferred_element_type=jnp.float32),
        "dp",
        scatter_dimension=0,
        tiled=True,
    )
    weighted = final_gain.astype(jnp.float32) * direction
    square_part, product_part = lax.psum(
        (jnp.sum(residual * residual, axis=1), jnp.sum(residual * weighted, axis=1)), "mp"
    )
    inverse = lax.rsqrt(square_part / MODEL_WIDTH + 1e-05)
    metric = inverse * product_part
    grad_last = (
        weighted * inverse[:, None] - residual * (metric * inverse * inverse / MODEL_WIDTH)[:, None]
    ).astype(jnp.bfloat16)
    grad_full = lax.all_gather(grad_last, "mp", axis=1, tiled=True)
    grad_seqs = lax.all_to_all(grad_full, "dp", split_axis=1, concat_axis=0, tiled=True)
    head_grads = lax.psum_scatter(
        lax.dot_general(
            grad_seqs, w_out, (((1,), (1,)), ((), ())), preferred_element_type=jnp.float32
        ),
        "dp",
        scatter_dimension=0,
        tiled=True,
    )
    mean_gap = head_mean[None, :] - last_out.astype(jnp.float32)
    scores = jnp.sum((mean_gap * head_grads).reshape(seq_count, q_heads, HEAD_SIZE), axis=2)
    return (head_out, scores, metric)


def solution(mesh):
    in_specs = (
        P("dp", "mp"),
        P(),
        P("dp", "mp"),
        P("dp", "mp"),
        P("dp", "mp"),
        P("mp", "dp"),
        P("mp"),
        P("dp", "mp"),
        P(),
        P(),
    )
    out_specs = (P("dp", "mp"), P("dp", "mp"), P("dp"))
    return jax.shard_map(
        per_device, mesh=mesh, in_specs=in_specs, out_specs=out_specs, check_vma=False
    )
```

profile of v0, /device:TPU:0, one launch (start us, length us, event | category | flops | bytes accessed | tf_op | source)
XLA Modules:
  0.0 371.3 jit_solution(14169582162044416903)
XLA Ops:
  7.2 0.7 all-gather.6.cloned.1.call-update
  7.9 0.0 all-gather.10.cloned.1.call-start
  8.0 0.7 all-gather.10.cloned.1.call-update
  8.7 0.7 all-gather.12.cloned.1.call-update
  9.4 0.5 all-gather.8.cloned.1.call-update
  10.0 0.0 all-reduce.6.cloned.1.call-start
  10.1 13.9 %fusion.15 = f32[8,2048]{1,0:T(8,128)} fusion(bf16[8016,2048]{1,0:T(8,128)(2,1)} %param.17, s32[8016]{0:T(1024)S(1)} %iota_add_fusion, s32[8]{0:T(128)} %param.19, s32[8]{0:T(128)} %param.18), kind=kOutput, calls=%fused_computation.31 | convolution fusion | flops 263053056 | bytes 32931200 | tf_op jit(solution)/shard_map/dot_general | solution.py:112
  24.1 0.5 fusion.14
  24.6 68.5 %all-gather.6.cloned.1.call-done = bf16[256,8192]{1,0:T(8,128)(2,1)} async-done(((bf16[256,2048]{1,0:T(8,128)(2,1)}), bf16[256,8192]{1,0:T(8,128)(2,1)}) %all-gather.6.cloned.1.call-update) | async-done | bytes 4194320 | tf_op jit(solution)/shard_map/all_gather | solution.py:47
  93.1 3.1 fusion
  96.2 25.1 %all-gather.10.cloned.1.call-done = bf16[8192,128]{1,0:T(8,128)(2,1)} async-done(((bf16[1024,128]{1,0:T(8,128)(2,1)}), bf16[8192,128]{1,0:T(8,128)(2,1)}) %all-gather.10.cloned.1.call-update) | async-done | bytes 2097168 | tf_op jit(solution)/shard_map/all_gather | solution.py:56
  121.2 4.6 %convolution_bitcast_fusion.1 = f32[1,256,1,128]{1,3,2,0:T(8,128)S(1)} fusion(bf16[8192,128]{1,0:T(8,128)(2,1)} %all-gather.10.cloned.1.call-done, bf16[256,8192]{1,0:T(8,128)(2,1)} %all-gather.6.cloned.1.call-done, f32[8192]{0:T(1024)S(1)} %convert_element_type.78, f32[256]{0:T(256)S(1)} %add_rsqrt_fusion), kind=kOutput, calls=%fused_computation.11 | convolution fusion | flops 545259520 | bytes 6456320 | tf_op jit(solution)/shard_map/dot_general | solution.py:61
  125.9 0.3 fusion.23
  126.2 86.7 %all-gather.12.cloned.1.call-done = bf16[8192,1024]{1,0:T(8,128)(2,1)} async-done(((bf16[1024,1024]{1,0:T(8,128)(2,1)}), bf16[8192,1024]{1,0:T(8,128)(2,1)}) %all-gather.12.cloned.1.call-update) | async-done | bytes 16777232 | tf_op jit(solution)/shard_map/all_gather | solution.py:55
  212.9 9.5 %convolution_bitcast_fusion = f32[32,8,8,128]{3,1,2,0:T(8,128)S(1)} fusion(bf16[8192,1024]{1,0:T(8,128)(2,1)} %all-gather.12.cloned.1.call-done, bf16[256,8192]{1,0:T(8,128)(2,1)} %all-gather.6.cloned.1.call-done, f32[8192]{0:T(1024)S(1)} %convert_element_type.78, f32[256]{0:T(256)S(1)} %add_rsqrt_fusion), kind=kOutput, calls=%fused_computation.9 | convolution fusion | flops 4303355904 | bytes 22053888 | tf_op jit(solution)/shard_map/dot_general | solution.py:61
  222.4 0.2 copy.52
  222.6 0.3 fusion.38
  222.9 0.4 fusion.8
  223.3 0.7 fusion.39
  224.0 1.3 copy-done.1
  225.4 0.3 fusion.3
  225.7 16.7 %all-gather.8.cloned.1.call-done = bf16[8192,128]{1,0:T(8,128)(2,1)} async-done(((bf16[1024,128]{1,0:T(8,128)(2,1)}), bf16[8192,128]{1,0:T(8,128)(2,1)}) %all-gather.8.cloned.1.call-update) | async-done | bytes 2097168 | tf_op jit(solution)/shard_map/all_gather | solution.py:57
  242.4 5.4 %convert_reduce_fusion = (f32[8,128]{1,0:T(8,128)S(1)}, bf16[128,8,256]{2,0,1:T(8,128)(2,1)S(1)}) fusion(f32[8,256]{1,0:T(8,128)S(1)} %fusion.3, f32[1,1,8,256,256]{3,4,2,1,0:T(8,128)} %copy-done.1, f32[8,256]{1,0:T(8,128)S(1)} %get-tuple-element.30, bf16[8192,128]{1,0:T(8,128)(2,1)} %all-gather.8.cloned.1.call-done, ...), kind=kOutput, calls=%fused_computation.17 | convolution fusion | flops 681868288 | bytes 8967168 | tf_op jit(solution)/shard_map/bkgts,bskd->btkgd/dot_general | solution.py:86
  247.9 0.1 slice.28
  248.0 0.1 copy.51
  248.1 9.2 %all-gather = bf16[8,1,1024]{2,1,0:T(2,128)(2,1)S(1)} all-gather(bf16[1,1,1024]{2,1,0:T(2,128)(2,1)S(1)} %copy.51), channel_id=2, replica_groups=mesh['dp'=8,'mp'=4] {'dp'}, dimensions={0}, use_global_device_ids=true | all-gather | bytes 18432 | tf_op jit(solution)/shard_map/all_gather | solution.py:96
  257.4 0.4 fusion.5
  257.8 18.7 %psum.29 = bf16[8,1,1024]{2,0,1:T(8,128)(2,1)S(1)} all-reduce(bf16[8,1,1024]{2,0,1:T(8,128)(2,1)S(1)} %fusion.5), channel_id=1, replica_groups=mesh['dp'=8,'mp'=4] {'mp'}, use_global_device_ids=true, to_apply=%region_6.7 | all-reduce | flops 8192 | bytes 32768 | tf_op jit(solution)/shard_map/psum | solution.py:98
  276.5 0.5 broadcast.94
  277.0 0.6 reduce.6
  277.6 0.6 reshape.224
  278.2 3.3 all-to-all-start
  281.6 0.6 dynamic-slice
  282.1 4.0 %all-to-all-done = bf16[8,2,512]{2,1,0:T(2,128)(2,1)S(1)} async-done(((bf16[8,2,512]{2,1,0:T(2,128)(2,1)}), bf16[8,2,512]{2,1,0:T(2,128)(2,1)S(1)}, u32[]{:S(2)}, u32[]{:S(2)}) %all-to-all-start) | async-done | bytes 16416 | tf_op jit(solution)/shard_map/all_to_all | solution.py:99
  286.2 13.0 %all-reduce.6.cloned.1.call-done = f32[8,2048]{1,0:T(8,128)} async-done(((f32[8,2048]{1,0:T(8,128)}), f32[8,2048]{1,0:T(8,128)}) %all-reduce.6.cloned.1.call-update) | async-done | bytes 65552
  299.2 2.1 multiply_reduce_fusion
  301.4 12.3 %all-reduce.3 = (f32[1]{0:T(128)}, f32[1]{0:T(128)}) all-reduce(f32[1]{0:T(128)} %bitcast.23, f32[1]{0:T(128)} %bitcast.25), channel_id=1, replica_groups=mesh['dp'=8,'mp'=4] {'mp'}, use_global_device_ids=true, to_apply=%region_8.9 | all-reduce | flops 2 | bytes 16 | tf_op jit(solution)/shard_map/psum | solution.py:118
  315.0 1.5 subtract_convert_fusion.4
  316.5 13.1 %all_gather.23 = bf16[1,8192]{1,0:T(2,128)(2,1)S(1)} all-gather(bf16[1,2048]{1,0:T(2,128)(2,1)S(1)} %subtract_convert_fusion.4), channel_id=1, replica_groups=mesh['dp'=8,'mp'=4] {'mp'}, dimensions={1}, use_global_device_ids=true | all-gather | bytes 20480 | tf_op jit(solution)/shard_map/all_gather | solution.py:126
  329.7 0.6 reduce.7
  330.3 0.6 reshape.226
  330.9 3.3 all-to-all-start.1
  334.3 1.0 copy.41
  335.3 3.7 all-to-all-done.1
  339.0 0.6 fusion.25
  339.6 22.8 %all-reduce.2 = (f32[1024]{0:T(1024)S(1)}, f32[8,1024]{1,0:T(8,128)S(1)}) all-reduce(f32[1024]{0:T(1024)S(1)} %bitcast.92, f32[8,1024]{1,0:T(8,128)S(1)} %fusion.25), channel_id=1, replica_groups=mesh['dp'=8,'mp'=4] {'dp'}, use_global_device_ids=true, to_apply=%region_4.5 | all-reduce | flops 9216 | bytes 73728 | tf_op jit(solution)/shard_map/psum | solution.py:91
  362.4 0.7 dynamic-slice_multiply_fusion.1
  363.0 0.6 reduce_sum.70
  (23 shorter events, 0.3 us)
Async XLA Ops:
  7.2 250.2 %copy-start = (bf16[1024,1024]{1,0:T(8,128)(2,1)S(1)}, bf16[1024,1024]{1,0:T(8,128)(2,1)}, u32[]{:S(2)}) copy-start(bf16[1024,1024]{1,0:T(8,128)(2,1)} %param.15) | copy-start | bytes 6291460
  7.2 85.9 %all-gather.6.cloned.1.call-start = ((), (), s32[]{:S(2)}) async-start(), calls=%async_computation.2 | async-start | bytes 5242880 | tf_op jit(solution)/shard_map/all_gather | solution.py:47
  7.9 113.3 %all-gather.10.cloned.1.call-start = ((), (), s32[]{:S(2)}) async-start(), calls=%async_computation.4 | async-start | bytes 2359296 | tf_op jit(solution)/shard_map/all_gather | solution.py:56
  8.7 204.2 %all-gather.12.cloned.1.call-start = ((), (), s32[]{:S(2)}) async-start(), calls=%async_computation.5 | async-start | bytes 18874368 | tf_op jit(solution)/shard_map/all_gather | solution.py:55
  9.4 233.0 %all-gather.8.cloned.1.call-start = ((), (), s32[]{:S(2)}) async-start(), calls=%async_computation.3 | async-start | bytes 2359296 | tf_op jit(solution)/shard_map/all_gather | solution.py:57
  10.0 289.3 %all-reduce.6.cloned.1.call-start = ((), (), s32[]{:S(2)}) async-start(), calls=%async_computation.6 | async-start | bytes 131072
  10.0 14.0 %copy-start.2 = (bf16[8192]{0:T(1024)(128)(2,1)S(1)}, bf16[8192]{0:T(1024)(128)(2,1)}, u32[]{:S(2)}) copy-start(bf16[8192]{0:T(1024)(128)(2,1)} %param.11) | copy-start | bytes 49156
  224.0 1.4 copy-start.1
  225.7 55.8 %copy-start.3 = (bf16[2048]{0:T(1024)(128)(2,1)S(1)}, bf16[2048]{0:T(1024)(128)(2,1)}, u32[]{:S(2)}) copy-start(bf16[2048]{0:T(1024)(128)(2,1)} %param.16) | copy-start | bytes 12292
  225.7 55.9 %copy-start.4 = (u32[32]{0:T(128)S(1)}, u32[32]{0:T(128)}, u32[]{:S(2)}) copy-start(u32[32]{0:T(128)} %constant.44) | copy-start | bytes 388
  278.2 8.0 %all-to-all-start = ((bf16[8,2,512]{2,1,0:T(2,128)(2,1)}), bf16[8,2,512]{2,1,0:T(2,128)(2,1)S(1)}, u32[]{:S(2)}, u32[]{:S(2)}) async-start(bf16[8,2,512]{2,1,0:T(2,128)(2,1)} %reshape.224), calls=%async_computation | async-start | bytes 32768 | tf_op jit(solution)/shard_map/all_to_all | solution.py:99
  330.9 8.0 %all-to-all-start.1 = ((bf16[8,2,512]{2,1,0:T(2,128)(2,1)}), bf16[8,2,512]{2,1,0:T(2,128)(2,1)S(1)}, u32[]{:S(2)}, u32[]{:S(2)}) async-start(bf16[8,2,512]{2,1,0:T(2,128)(2,1)} %reshape.226), calls=%async_computation.1 | async-start | bytes 32768 | tf_op jit(solution)/shard_map/all_to_all | solution.py:127
Sparse Core Ops, SparseCore 0:
  9.6 83.4 all-gather.5
  94.9 26.2 all-gather.9
  123.1 89.7 all-gather.11
  214.6 27.7 all-gather.7
  245.9 53.2 all-reduce.5
where the time goes:
time: 372 us; the launch traced here: 371 us
  waiting for transfers between devices  220 us (59%)
  blocking collectives  76.2 us (20%)
  matrix products  35.1 us (9%)
  between operations  16.5 us (4%)
  other arithmetic  10.8 us (3%)
  starting transfers between devices  6.86 us (2%)
  local copies, waits for them, and re-layouts  5.52 us (1%)
    all_gather x1, waiting for transfers between devices, per_device(): lax.all_gather(w_query, 'dp', axis=0, tiled=True)  86.7 us
    all_gather x1, waiting for transfers between devices, per_device(): gathered = lax.all_gather(tokens, 'mp', axis=1, tiled=True)  68.5 us
    all_gather x1, waiting for transfers between devices, per_device(): lax.all_gather(key_projection_weight, 'dp', axis=0, tiled=True)  25.1 us
    psum x1, blocking collectives, per_device(): all_totals = lax.psum(totals, 'dp')  22.8 us
    psum x1, blocking collectives, per_device(): summed_out = lax.psum(partial_out.astype(jnp.bfloat16), 'mp')  18.7 us
    all_gather x1, waiting for transfers between devices, per_device(): lax.all_gather(value_projection_weight, 'dp', axis=0, tiled=True)  16.7 us
    unnamed x6, waiting for transfers between devices  15.6 us
    dot_general x2, matrix products, per_device(): jnp.dot(normalized_rows, weight_piece, preferred_element_type=jnp.float32)  14.1 us
  transfers between devices with their start and end apart: 7, of which 7 were waited for; matrix products, arithmetic and copies ran while one was open for 12% of the time, Pallas kernels for 0%

commit v1 on v0

v1 whole, which is shorter than its diff:
```python
import functools
import math

import jax
import jax.numpy as jnp
from jax import lax
from jax.experimental import pallas as pl
from jax.experimental.pallas import tpu as pltpu
from jax.sharding import PartitionSpec as P

HEAD_SIZE = 128
SEQUENCE_LENGTH = 256
MESH = pl.DeviceIdType.MESH
F32 = jnp.float32
BF16 = jnp.bfloat16


def flip(index, mask):
    bit = 1
    out = index
    while bit <= mask:
        if mask & bit:
            out = out + bit - 2 * bit * ((index // bit) % 2)
        bit *= 2
    return out


def spread_plan(size):
    bits = []
    bit = 2
    while bit < size:
        bits.append(bit)
        bit *= 2
    parts = min(2, len(bits))
    plan = []
    for part in range(parts):
        order = bits[part:] + bits[:part]
        held = [0]
        arrivals = []
        for step, b in enumerate(order):
            fresh = [h ^ b for h in held]
            arrivals += [(f, step) for f in fresh]
            held = held + fresh
        plan.append((order, arrivals))
    return plan


def project_kernel(
    D, M, chunks, xchunks,
    tok_ref, gain_ref, wq_ref, wk_ref, wv_ref, out_ref,
    x_all, w_all, loc_sem, xloc_sem, xs_sem, xr_sem, ps_sem, pr_sem, cs_sem, cr_sem,
):
    d = lax.axis_index("dp")
    m = lax.axis_index("mp")
    plan = spread_plan(D)
    parts = len(plan)
    n_bits = D.bit_length() - 1
    depth = wq_ref.shape[0]
    rows = tok_ref.shape[0]
    width = tok_ref.shape[1]
    qw, kw, vw = wq_ref.shape[1], wk_ref.shape[1], wv_ref.shape[1]
    piece = depth // (parts * chunks)
    xpiece = rows // xchunks

    def wrows(p, c):
        return pl.ds((p * chunks + c) * piece, piece)

    own = []
    for c in range(chunks):
        for p in range(parts):
            rr = wrows(p, c)
            trio = []
            for i, (src, lo, n) in enumerate(
                ((wq_ref, 0, qw), (wk_ref, qw, kw), (wv_ref, qw + kw, vw))
            ):
                cp = pltpu.make_async_copy(
                    src.at[rr, :], w_all.at[d, rr, pl.ds(lo, n)], loc_sem.at[p, c, i]
                )
                cp.start()
                trio.append(cp)
            own.append((p, c, trio))
    xown = pltpu.make_async_copy(tok_ref, x_all.at[m], xloc_sem)
    xown.start()

    barrier = pltpu.get_barrier_semaphore()
    for b in range(n_bits):
        pl.semaphore_signal(barrier, inc=1, device_id=(flip(d, 1 << b), m), device_id_type=MESH)

    @pl.when(m > 0)
    def _():
        pl.semaphore_signal(barrier, inc=1, device_id=(d, m - 1), device_id_type=MESH)

    @pl.when(m < M - 1)
    def _():
        pl.semaphore_signal(barrier, inc=1, device_id=(d, m + 1), device_id_type=MESH)

    pl.semaphore_wait(barrier, n_bits + jnp.where(m > 0, 1, 0) + jnp.where(m < M - 1, 1, 0))

    def xsend(hop, c, side):
        rr = pl.ds(c * xpiece, xpiece)
        owner = m - hop if side == 0 else m + hop
        to = m + 1 if side == 0 else m - 1
        return pltpu.make_async_remote_copy(
            src_ref=(tok_ref.at[rr, :] if hop == 0 else x_all.at[owner, rr, :]),
            dst_ref=x_all.at[owner, rr, :],
            send_sem=xs_sem.at[hop, c, side],
            recv_sem=xr_sem.at[hop, c, side],
            device_id=(d, to),
            device_id_type=MESH,
        )

    def xpred(hop, side):
        if side == 0:
            return (m < M - 1) & (m - hop >= 0)
        return (m > 0) & (m + hop < M)

    def xstart(hop, c):
        for side in range(2):
            @pl.when(xpred(hop, side))
            def _(side=side):
                xsend(hop, c, side).start()

    def xwait(hop, c):
        rr = pl.ds(c * xpiece, xpiece)
        for side in range(2):
            owner = m - hop - 1 if side == 0 else m + hop + 1
            ok = (m - hop - 1 >= 0) if side == 0 else (m + hop + 1 < M)

            @pl.when(ok)
            def _(side=side, owner=owner):
                pltpu.make_async_copy(
                    x_all.at[owner, rr, :], x_all.at[owner, rr, :], xr_sem.at[hop, c, side]
                ).wait()

    for c in range(xchunks):
        xstart(0, c)

    sends = []

    def wcopy(mask, p, c, bit, send_sem, recv_sem):
        owner = flip(d, mask)
        rr = wrows(p, c)
        return pltpu.make_async_remote_copy(
            src_ref=w_all.at[owner, rr, :],
            dst_ref=w_all.at[owner, rr, :],
            send_sem=send_sem,
            recv_sem=recv_sem,
            device_id=(flip(d, bit), m),
            device_id_type=MESH,
        )

    def wsend(mask, p, c, step):
        bit = plan[p][0][step]
        cp = wcopy(mask, p, c, bit, ps_sem.at[p, mask // 2, c, step],
                   pr_sem.at[p, (mask ^ bit) // 2, c])
        cp.start()
        sends.append(cp)

    def csend(mask, p, c):
        cp = wcopy(mask, p, c, 1, cs_sem.at[p, mask // 2, c], cr_sem.at[p, mask // 2, c])
        cp.start()
        sends.append(cp)

    def wwait(mask, p, c, sem):
        owner = flip(d, mask)
        rr = wrows(p, c)
        pltpu.make_async_copy(w_all.at[owner, rr, :], w_all.at[owner, rr, :], sem).wait()

    steps = len(plan[0][0])
    for p, c, trio in own:
        for cp in trio:
            cp.wait()
        wsend(0, p, c, 0)
    for step in range(1, steps):
        for c in range(chunks):
            for p in range(parts):
                wsend(0, p, c, step)
    for c in range(chunks):
        for p in range(parts):
            csend(0, p, c)

    rounds = len(plan[0][1])
    wevents = [(r, c) for r in range(rounds) for c in range(chunks)]
    xevents = [(h, c) for h in range(M - 1) for c in range(xchunks)]
    merged = sorted(
        [((i + 1) / len(wevents), 1, e) for i, e in enumerate(wevents)]
        + [(0.8 * (i + 1) / len(xevents), 0, e) for i, e in enumerate(xevents)]
    )

    def take(r, c):
        for p in range(parts):
            mask, step = plan[p][1][r]
            wwait(mask, p, c, pr_sem.at[p, mask // 2, c])
            for later in range(step + 1, steps):
                wsend(mask, p, c, later)
            csend(mask, p, c)

    def use(owner, lo, n):
        base = owner * depth
        shard = base // width
        col = pl.multiple_of(base % width + lo, 128 if n % 128 == 0 else n)
        out_ref[...] += jnp.dot(
            x_all[shard, :, pl.ds(col, n)], w_all[owner, pl.ds(lo, n), :],
            preferred_element_type=F32,
        )

    x_left = len(xevents)
    for _, kind, (a, c) in merged:
        if kind == 0:
            xwait(a, c)
            if a + 1 < M - 1:
                xstart(a + 1, c)
            x_left -= 1
            if x_left == 0:
                xown.wait()
                total = jnp.zeros((rows, 1), F32)
                for k in range(M):
                    xv = x_all[k].astype(F32)
                    total = total + jnp.sum(xv * xv, axis=1, keepdims=True)
                inv = lax.rsqrt(total / (M * width) + 1e-05)
                for h in range(M - 1):
                    for cc in range(xchunks):
                        for side in range(2):
                            @pl.when(xpred(h, side))
                            def _(h=h, cc=cc, side=side):
                                xsend(h, cc, side).wait_send()
                for k in range(M):
                    g = gain_ref[:, k * width:(k + 1) * width].astype(F32)
                    x_all[k] = (x_all[k].astype(F32) * inv * g).astype(BF16)
                out_ref[...] = jnp.zeros_like(out_ref)
        else:
            take(a, c)
    order = [0]
    for r in range(rounds):
        for p in range(parts):
            if plan[p][1][r][0] not in order:
                order.append(plan[p][1][r][0])
    for mask in order:
        use(flip(d, mask), 0, depth)
    for mask in order:
        for p in range(parts):
            for c in range(chunks):
                wwait(mask + 1, p, c, cr_sem.at[p, mask // 2, c])
        use(flip(d, mask + 1), 0, depth)
    for cp in sends:
        cp.wait_send()


def project(D, M, tokens, gain, wq, wk, wv):
    rows, width = tokens.shape
    depth = wq.shape[0]
    total = wq.shape[1] + wk.shape[1] + wv.shape[1]
    parts = len(spread_plan(D))
    steps = len(spread_plan(D)[0][0])
    chunks = 2 if depth // (2 * parts) >= 128 else 1
    xchunks = 2
    half = D // 2
    DMA = pltpu.SemaphoreType.DMA
    ANY = pl.BlockSpec(memory_space=pl.ANY)
    return pl.pallas_call(
        functools.partial(project_kernel, D, M, chunks, xchunks),
        name="project",
        out_shape=jax.ShapeDtypeStruct((rows, total), F32),
        in_specs=[ANY, pl.BlockSpec(memory_space=pltpu.VMEM), ANY, ANY, ANY],
        out_specs=pl.BlockSpec(memory_space=pltpu.VMEM),
        scratch_shapes=[
            pltpu.VMEM((M, rows, width), BF16),
            pltpu.VMEM((D, depth, total), BF16),
            DMA((parts, chunks, 3)),
            DMA(()),
            DMA((M - 1, xchunks, 2)),
            DMA((M - 1, xchunks, 2)),
            DMA((parts, half, chunks, steps)),
            DMA((parts, half, chunks)),
            DMA((parts, half, chunks)),
            DMA((parts, half, chunks)),
        ],
        compiler_params=pltpu.CompilerParams(
            collective_id=0, has_side_effects=True, vmem_limit_bytes=56 * 1024 * 1024
        ),
    )(tokens, gain, wq, wk, wv)


def attend_kernel(q_ref, k_ref, v_ref, cos_ref, sin_ref, out_ref, stat_ref):
    cos, sin = cos_ref[...], sin_ref[...]
    half = HEAD_SIZE // 2

    def rope(x):
        turned = jnp.concatenate([x[:, half:], x[:, :half]], axis=1)
        return (x * cos + turned * sin).astype(BF16)

    q, k = rope(q_ref[...]), rope(k_ref[...])
    v = v_ref[...].astype(BF16)
    length = q.shape[0]
    logits = lax.dot_general(
        q, k, (((1,), (1,)), ((), ())), preferred_element_type=F32
    ) / math.sqrt(HEAD_SIZE)
    at = lax.broadcasted_iota(jnp.int32, (length, length), 0)
    key_at = lax.broadcasted_iota(jnp.int32, (length, length), 1)
    logits = jnp.where(at >= key_at, logits, -1e30)
    top = jnp.max(logits, axis=1, keepdims=True)
    e = jnp.exp(logits - top)
    probs = (e / jnp.sum(e, axis=1, keepdims=True)).astype(BF16)
    mixed = jnp.dot(probs, v, preferred_element_type=F32).astype(BF16)
    out_ref[...] = mixed
    wide = mixed.astype(F32)
    stat_ref[0:1, :] = jnp.sum(wide, axis=0, keepdims=True)
    stat_ref[1:2, :] = wide[length - 1:length, :]


def attend(qkv, q_heads, kv_heads):
    rows = qkv.shape[0]
    S = rows // SEQUENCE_LENGTH
    group = q_heads // kv_heads
    half = HEAD_SIZE // 2
    inv_freq = jnp.exp(jnp.arange(half, dtype=F32) * (-2.0 * math.log(500000.0) / HEAD_SIZE))
    angles = jnp.arange(SEQUENCE_LENGTH, dtype=F32)[:, None] * inv_freq[None, :]
    c, s = jnp.cos(angles), jnp.sin(angles)
    cos = jnp.concatenate([c, c], axis=1)
    sin = jnp.concatenate([-s, s], axis=1)
    block = (SEQUENCE_LENGTH, HEAD_SIZE)
    table = pl.BlockSpec(block, lambda b, h: (0, 0))
    return pl.pallas_call(
        attend_kernel,
        name="attend",
        grid=(S, q_heads),
        in_specs=[
            pl.BlockSpec(block, lambda b, h: (b, h)),
            pl.BlockSpec(block, lambda b, h: (b, q_heads + h // group)),
            pl.BlockSpec(block, lambda b, h: (b, q_heads + kv_heads + h // group)),
            table,
            table,
        ],
        out_specs=[
            pl.BlockSpec(block, lambda b, h: (b, h)),
            pl.BlockSpec((None, 2, HEAD_SIZE), lambda b, h: (b, 0, h)),
        ],
        out_shape=[
            jax.ShapeDtypeStruct((rows, q_heads * HEAD_SIZE), BF16),
            jax.ShapeDtypeStruct((S, 2, q_heads * HEAD_SIZE), F32),
        ],
    )(qkv, qkv, qkv, cos, sin)


def tail_kernel(
    D, M, S, heads, token_count, model_width,
    stat_ref, wout_ref, contrib_ref, tok_ref, gain_ref, scores_ref, metric_ref,
    stat_all, rows_a, out_src, out_all, dir_all, sq_src, sq_all, g_src, g_all, hg_src, hg_all,
    s1, r1, s2, r2, s3, r3, s5, r5, s6, r6, s7, r7,
):
    d = lax.axis_index("dp")
    m = lax.axis_index("mp")
    R = D // M
    cols = wout_ref.shape[1]
    everyone = D * M
    me = d * M + m

    barrier = pltpu.get_barrier_semaphore()

    @pl.loop(1, everyone)
    def _(i):
        other = (me + i) % everyone
        pl.semaphore_signal(
            barrier, inc=1, device_id=(other // M, other % M), device_id_type=MESH
        )

    pl.semaphore_wait(barrier, everyone - 1)

    pending = []

    def remote(src, dst, ss, rs, to, cond=None):
        cp = pltpu.make_async_remote_copy(
            src_ref=src, dst_ref=dst, send_sem=ss, recv_sem=rs, device_id=to, device_id_type=MESH
        )
        if cond is None:
            cp.start()
        else:
            pl.when(cond)(cp.start)
        pending.append((cp, cond))

    def local(src, dst, rs, cond=None):
        cp = pltpu.make_async_copy(src, dst, rs)
        if cond is None:
            cp.start()
        else:
            pl.when(cond)(cp.start)

    def arrive(buf, sem, n):
        for i in range(n):
            pltpu.make_async_copy(buf.at[i], buf.at[i], sem.at[i]).wait()

    for i in range(1, D):
        to = (d + i) % D
        remote(stat_ref, stat_all.at[d], s1.at[i], r1.at[d], (to, m))
    local(stat_ref, stat_all.at[d], r1.at[d])
    for i in range(1, D):
        to = (d + i) % D
        remote(contrib_ref.at[to], dir_all.at[d], s2.at[i], r2.at[d], (to, m))
    local(contrib_ref.at[d], dir_all.at[d], r2.at[d])

    arrive(stat_all, r1, D)
    for j in range(D):
        for b in range(S):
            rows_a[j * S + b:j * S + b + 1, :] = stat_all[j, 2 * b + 1:2 * b + 2, :]
    w = wout_ref[...]
    partial = jnp.dot(rows_a[...].astype(BF16), w, preferred_element_type=F32)
    for j in range(D):
        out_src[j] = partial[j * S:(j + 1) * S, :]
    span = d // R
    slot = (d % R) * M + m
    for i in range(D):
        to = (d + i) % D
        if i == 0:
            remote(out_src.at[to], out_all.at[slot], s3.at[i], r3.at[slot], (to, span), m != span)
            local(out_src.at[to], out_all.at[slot], r3.at[slot], m == span)
        else:
            remote(out_src.at[to], out_all.at[slot], s3.at[i], r3.at[slot], (to, span))

    mean = jnp.zeros((1, stat_all.shape[2]), F32)
    for j in range(D):
        for b in range(S):
            mean = mean + stat_all[j, 2 * b:2 * b + 1, :]
    mean = mean / token_count
    arrive(dir_all, r2, D)
    direction = dir_all[0]
    for j in range(1, D):
        direction = direction + dir_all[j]
    weighted = gain_ref[...].astype(F32) * direction

    arrive(out_all, r3, D)
    pieces = []
    for jj in range(R):
        acc = out_all[jj * M]
        for k in range(1, M):
            acc = acc + out_all[jj * M + k]
        pieces.append(acc)
    attn_last = jnp.concatenate(pieces, axis=1).astype(BF16).astype(F32)
    residual = tok_ref[...].astype(F32) + attn_last
    sq_src[0] = jnp.broadcast_to(jnp.sum(residual * residual, axis=1, keepdims=True), (S, 128))
    sq_src[1] = jnp.broadcast_to(jnp.sum(residual * weighted, axis=1, keepdims=True), (S, 128))
    for i in range(1, M):
        to = (m + i) % M
        remote(sq_src, sq_all.at[m], s5.at[i], r5.at[m], (d, to))
    local(sq_src, sq_all.at[m], r5.at[m])
    arrive(sq_all, r5, M)
    square = sq_all[0, 0]
    product = sq_all[0, 1]
    for k in range(1, M):
        square = square + sq_all[k, 0]
        product = product + sq_all[k, 1]
    inverse = lax.rsqrt(square / model_width + 1e-05)
    metric = inverse * product
    metric_ref[...] = metric[:, 0:1]
    grad = weighted * inverse[:, 0:1] - residual * (
        metric * inverse * inverse / model_width
    )[:, 0:1]
    for jj in range(R):
        g_src[jj] = grad[:, jj * cols:(jj + 1) * cols].astype(BF16).astype(F32)
    for jj in range(R):
        to = m * R + jj
        for i in range(M):
            k = (m + i) % M
            if i == 0:
                remote(g_src.at[jj], g_all.at[d], s6.at[jj, i], r6.at[d], (to, k), to != d)
                local(g_src.at[jj], g_all.at[d], r6.at[d], to == d)
            else:
                remote(g_src.at[jj], g_all.at[d], s6.at[jj, i], r6.at[d], (to, k))
    arrive(g_all, r6, D)
    for j in range(D):
        rows_a[j * S:(j + 1) * S, 0:cols] = g_all[j]
    hg = lax.dot_general(
        rows_a[:, 0:cols].astype(BF16), w, (((1,), (1,)), ((), ())), preferred_element_type=F32
    )
    for j in range(D):
        hg_src[j] = hg[j * S:(j + 1) * S, :]
    for i in range(1, D):
        to = (d + i) % D
        remote(hg_src.at[to], hg_all.at[d], s7.at[i], r7.at[d], (to, m))
    local(hg_src.at[d], hg_all.at[d], r7.at[d])
    arrive(hg_all, r7, D)
    grads = hg_all[0]
    for j in range(1, D):
        grads = grads + hg_all[j]
    lasts = [stat_ref[2 * b + 1:2 * b + 2, :] for b in range(S)]
    last = lasts[0] if S == 1 else jnp.concatenate(lasts, axis=0)
    gap = (mean - last) * grads
    lane = lax.broadcasted_iota(jnp.int32, (S, heads), 1)
    scores = jnp.zeros((S, heads), F32)
    for h in range(heads):
        part = jnp.sum(gap[:, h * HEAD_SIZE:(h + 1) * HEAD_SIZE], axis=1, keepdims=True)
        scores = jnp.where(lane == h, part, scores)
    scores_ref[...] = scores
    for cp, cond in pending:
        if cond is None:
            cp.wait_send()
        else:
            pl.when(cond)(cp.wait_send)


def tail(D, M, stat, w_out, contrib, last_tokens, final_gain, token_count):
    S = stat.shape[0]
    entries, cols = w_out.shape
    width = last_tokens.shape[1]
    heads = entries // HEAD_SIZE
    R = D // M
    DMA = pltpu.SemaphoreType.DMA
    V = pl.BlockSpec(memory_space=pltpu.VMEM)
    wide = max(entries, cols)
    return pl.pallas_call(
        functools.partial(tail_kernel, D, M, S, heads, token_count, cols * D),
        name="tail",
        out_shape=[jax.ShapeDtypeStruct((S, heads), F32), jax.ShapeDtypeStruct((S, 1), F32)],
        in_specs=[V] * 5,
        out_specs=[V, V],
        scratch_shapes=[
            pltpu.VMEM((D, 2 * S, entries), F32),
            pltpu.VMEM((D * S, wide), F32),
            pltpu.VMEM((D, S, cols), F32),
            pltpu.VMEM((D, S, cols), F32),
            pltpu.VMEM((D, S, width), F32),
            pltpu.VMEM((2, S, 128), F32),
            pltpu.VMEM((M, 2, S, 128), F32),
            pltpu.VMEM((R, S, cols), F32),
            pltpu.VMEM((D, S, cols), F32),
            pltpu.VMEM((D, S, entries), F32),
            pltpu.VMEM((D, S, entries), F32),
            DMA((D,)), DMA((D,)), DMA((D,)), DMA((D,)), DMA((D,)), DMA((D,)),
            DMA((M,)), DMA((M,)), DMA((R, M)), DMA((D,)), DMA((D,)), DMA((D,)),
        ],
        compiler_params=pltpu.CompilerParams(
            collective_id=1, has_side_effects=True, vmem_limit_bytes=32 * 1024 * 1024
        ),
    )(stat.reshape(2 * S, entries), w_out, contrib, last_tokens, final_gain.reshape(1, width))


def per_device(
    D, M, tokens, attn_gain, w_query, key_w, value_w, w_out, final_gain, unembed,
    clean_ids, corrupt_ids,
):
    S = tokens.shape[0] // SEQUENCE_LENGTH
    vocab_rows, width = unembed.shape
    start = lax.axis_index("dp") * vocab_rows

    def picked(ids):
        at = ids - start
        ok = (at >= 0) & (at < vocab_rows)
        rows = jnp.take(unembed, jnp.clip(at, 0, vocab_rows - 1), axis=0)
        return jnp.where(ok[:, None], rows.astype(F32), 0.0)

    contrib = (picked(clean_ids) - picked(corrupt_ids)).reshape(D, S, width)
    qkv = project(D, M, tokens, attn_gain.reshape(1, -1), w_query, key_w, value_w)
    q_heads = w_query.shape[1] // HEAD_SIZE
    kv_heads = key_w.shape[1] // HEAD_SIZE
    head_out, stat = attend(qkv, q_heads, kv_heads)
    last_tokens = tokens.reshape(S, SEQUENCE_LENGTH, width)[:, SEQUENCE_LENGTH - 1, :]
    scores, metric = tail(
        D, M, stat, w_out, contrib, last_tokens, final_gain, tokens.shape[0] * D
    )
    return head_out, scores, metric.reshape(S)


def solution(mesh):
    in_specs = (
        P("dp", "mp"), P(), P("dp", "mp"), P("dp", "mp"), P("dp", "mp"),
        P("mp", "dp"), P("mp"), P("dp", "mp"), P(), P(),
    )
    out_specs = (P("dp", "mp"), P("dp", "mp"), P("dp"))
    return jax.shard_map(
        functools.partial(per_device, mesh.shape["dp"], mesh.shape["mp"]),
        mesh=mesh, in_specs=in_specs, out_specs=out_specs, check_vma=False,
    )
```

time: 372 us -> 147 us (0.40)
  waiting for transfers between devices: 220 us -> 0 us
  Pallas kernels: 0 us -> 132 us
  blocking collectives: 76.2 us -> 0 us
  matrix products: 35.1 us -> 0 us
  between operations: 16.5 us -> 2.51 us
  other arithmetic: 10.8 us -> 2.13 us
  starting transfers between devices: 6.86 us -> 0 us
    all_gather x4 -> x0, waiting for transfers between devices: 197 us -> none  [the longest x1 86.7 us: per_device(): lax.all_gather(w_query, 'dp', axis=0, tiled=True)]
    pallas_call x0 -> x3, Pallas kernels: none -> 132 us  [the longest x1 99.2 us: project(): pl.pallas_call(functools.partial(project_kernel, D, M, chunks, xchunks),...]
    psum x3 -> x0, blocking collectives: 53.8 us -> none  [the longest x1 22.8 us: per_device(): all_totals = lax.psum(totals, 'dp')]
    dot_general x7 -> x0, matrix products: 35.1 us -> none  [the longest x2 14.1 us: per_device(): jnp.dot(normalized_rows, weight_piece, preferred_element_type=jnp.float32)]
    all_gather x2 -> x0, blocking collectives: 22.4 us -> none  [the longest x1 13.1 us: per_device(): grad_full = lax.all_gather(grad_last, 'mp', axis=1, tiled=True)]
    unnamed x6 -> x0, waiting for transfers between devices: 15.6 us -> none
    all_to_all x2 -> x0, waiting for transfers between devices: 7.72 us -> none  [the longest x1 4.05 us: per_device(): lax.all_to_all(summed_out, 'dp', split_axis=0, concat_axis=1, tiled=True)]
    all_to_all x2 -> x0, starting transfers between devices: 6.67 us -> none  [the longest x1 3.33 us: per_device(): lax.all_to_all(grad_full, 'dp', split_axis=1, concat_axis=0, tiled=True)]
  transfers between devices with their start and end apart: 7 -> 0, of which waited for: 7 -> 0; matrix products, arithmetic and copies ran while one was open for 12% -> 0% of each run, Pallas kernels for 0% -> 0%
where the time goes in v1:
time: 147 us; the launch traced here: 146 us
  Pallas kernels  132 us (90%)
  local copies, waits for them, and re-layouts  8.73 us (6%)
  between operations  2.51 us (2%)
  other arithmetic  2.13 us (1%)
    pallas_call x1, Pallas kernels, project(): pl.pallas_call(functools.partial(project_kernel, D, M, chunks, xchunks),...  99.2 us
    pallas_call x1, Pallas kernels, tail(): pl.pallas_call(functools.partial(tail_kernel, D, M, S, heads, token_count...  25.4 us
    pallas_call x1, Pallas kernels, attend(): pl.pallas_call(attend_kernel, name='attend', grid=(S, q_heads), in_specs=...  7.83 us
    gather x2, local copies, waits for them, and re-layouts, picked(): rows = jnp.take(unembed, jnp.clip(at, 0, vocab_rows - 1), axis=0)  3.07 us

profile of v1, /device:TPU:0, one launch (start us, length us, event | category | flops | bytes accessed | tf_op | source)
XLA Modules:
  0.0 145.8 jit_solution(14308306665490419121)
XLA Ops:
  0.6 1.4 reshape.36.gain_ref
  2.0 99.2 %project.1.q_ref.k_ref.v_ref = f32[256,1280]{1,0:T(8,128)} custom-call(bf16[256,2048]{1,0:T(8,128)(2,1)} %tok_ref.1, bf16[1,8192]{1,0:T(2,128)(2,1)} %reshape.36.gain_ref, bf16[1024,1024]{1,0:T(8,128)(2,1)} %wq_ref.1, bf16[1024,128]{1,0:T(8,128)(2,1)} %wk_ref.1, bf16[1024,128]{1,0:T(8,128)(2,1)} %wv_ref.1), custom_call_target="tpu_custom_call" | custom-call | tf_op jit(solution)/shard_map/project/pallas_call | solution.py:260
  101.2 0.5 fusion.2
  101.8 0.8 pad_maximum_fusion
  102.6 7.8 %attend.1 = (bf16[256,1024]{1,0:T(8,128)(2,1)}, f32[1,2,1024]{2,1,0:T(2,128)}) custom-call(f32[256,1280]{1,0:T(8,128)} %project.1.q_ref.k_ref.v_ref, f32[256,1280]{1,0:T(8,128)} %project.1.q_ref.k_ref.v_ref, f32[256,1280]{1,0:T(8,128)} %project.1.q_ref.k_ref.v_ref, f32[256,128]{1,0:T(8,128)} %get-tuple-element.21.cos_ref, f32[256,128]{1,0:T(8,128)} %get-tuple-element.22.sin_ref), custom_call_target="tpu_custom_call" | custom-call | tf_op jit(solution)/shard_map/attend/pallas_call | solution.py:323
  110.4 0.7 compare_and_fusion
  111.1 1.5 %gather_fusion.1 = bf16[8,2048]{1,0:T(8,128)(2,1)S(1)} fusion(bf16[8016,2048]{1,0:T(8,128)(2,1)} %param.19, s32[1024]{0:T(1024)S(1)} %pad_clamp_fusion), kind=kCustom, calls=%fused_computation.1.clone | custom fusion | bytes 65568 | tf_op jit(solution)/shard_map/jit(_take)/gather | solution.py:547
  112.7 1.6 %gather_fusion = bf16[8,2048]{1,0:T(8,128)(2,1)S(1)} fusion(bf16[8016,2048]{1,0:T(8,128)(2,1)} %param.19, s32[1024]{0:T(1024)S(1)} %pad_clamp_fusion.1), kind=kCustom, calls=%fused_computation.clone | custom fusion | bytes 65568 | tf_op jit(solution)/shard_map/jit(_take)/gather | solution.py:547
  114.2 0.1 select_subtract_fusion
  114.3 0.8 slice_bitcast_fusion.tok_ref
  115.1 0.7 reshape.40.gain_ref
  115.8 0.0 copy-start
  115.8 1.6 %copy-done = bf16[1024,1024]{1,0:T(8,128)(2,1)S(1)} copy-done((bf16[1024,1024]{1,0:T(8,128)(2,1)S(1)}, bf16[1024,1024]{1,0:T(8,128)(2,1)}, u32[]{:S(2)}) %copy-start) | copy-done | bytes 2097176
  117.4 0.0 copy-start.1
  117.4 0.7 copy-done.1
  118.1 25.4 %tail.1 = (f32[1,8]{1,0:T(1,128)S(1)}, f32[1,1]{1,0:T(1,128)}) custom-call(f32[2,1024]{1,0:T(2,128)S(1)} %bitcast.5, bf16[1024,1024]{1,0:T(8,128)(2,1)S(1)} %copy-done, f32[8,1,2048]{2,1,0:T(1,128)S(1)} %reshape.38.contrib_ref, bf16[1,2048]{1,0:T(2,128)(2,1)S(1)} %slice_bitcast_fusion.tok_ref, bf16[1,2048]{1,0:T(2,128)(2,1)S(1)} %reshape.40.gain_ref), custom_call_target="tpu_custom_call" | custom-call | tf_op jit(solution)/shard_map/tail/pallas_call | solution.py:509
  143.5 0.5 copy.15
  (4 shorter events, 0.1 us)
Async XLA Ops:
  115.8 1.6 %copy-start = (bf16[1024,1024]{1,0:T(8,128)(2,1)S(1)}, bf16[1024,1024]{1,0:T(8,128)(2,1)}, u32[]{:S(2)}) copy-start(bf16[1024,1024]{1,0:T(8,128)(2,1)} %wout_ref.1) | copy-start | bytes 6291460
  117.4 0.7 copy-start.1

commit v2 on v1

v2 whole, which is shorter than its diff:
```python
import functools
import math

import jax
import jax.numpy as jnp
import numpy as np
from jax import lax
from jax.experimental import pallas as pl
from jax.experimental.pallas import tpu as pltpu
from jax.sharding import PartitionSpec as P

HEAD_SIZE = 128
SEQUENCE_LENGTH = 256
MESH = pl.DeviceIdType.MESH
F32 = jnp.float32
BF16 = jnp.bfloat16


def flip(index, mask):
    bit = 1
    out = index
    while bit <= mask:
        if mask & bit:
            out = out + bit - 2 * bit * ((index // bit) % 2)
        bit *= 2
    return out


def spread_plan(size):
    bits = []
    bit = 2
    while bit < size:
        bits.append(bit)
        bit *= 2
    parts = min(2, len(bits))
    plan = []
    for part in range(parts):
        order = bits[part:] + bits[:part]
        held = [0]
        arrivals = []
        for step, b in enumerate(order):
            fresh = [h ^ b for h in held]
            arrivals += [(f, step) for f in fresh]
            held = held + fresh
        plan.append((order, arrivals))
    return plan


def whole_kernel(
    D, M, chunks, xchunks, token_count,
    tok_ref, gain_ref, wq_ref, wk_ref, wv_ref, cos_hbm, sin_hbm, wout_hbm, contrib_ref, fgain_ref,
    head_ref, scores_ref, metric_ref,
    x_all, w_all, acc, cos_ref, sin_ref, wout_ref, tail_tok, q_s, k_s, v_s, tot_src,
    last_src, tot_all, last_all, rows_a, out_src, out_all, dir_all, sq_src, sq_all,
    g_src, g_all, hg_src, hg_all,
    loc_sem, one_sem, xs_sem, xr_sem, ps_sem, pr_sem, cs_sem, cr_sem,
    s1, r1, s2, r2, s3, r3, s4, r4, s5, r5, s6, r6, s7, r7,
):
    d = lax.axis_index("dp")
    m = lax.axis_index("mp")
    plan = spread_plan(D)
    parts = len(plan)
    depth = wq_ref.shape[0]
    rows, width = tok_ref.shape
    qw, kw, vw = wq_ref.shape[1], wk_ref.shape[1], wv_ref.shape[1]
    piece = depth // (parts * chunks)
    xpiece = rows // xchunks
    L = SEQUENCE_LENGTH
    S = rows // L
    heads, kv_heads = qw // HEAD_SIZE, kw // HEAD_SIZE
    G = heads // kv_heads
    cols = wout_ref.shape[1]
    R = D // M
    everyone = D * M
    me = d * M + m
    model_width = M * width

    def wrows(p, c):
        return pl.ds((p * chunks + c) * piece, piece)

    own = []
    for c in range(chunks):
        for p in range(parts):
            rr = wrows(p, c)
            trio = []
            for i, (src, lo, n) in enumerate(
                ((wq_ref, 0, qw), (wk_ref, qw, kw), (wv_ref, qw + kw, vw))
            ):
                cp = pltpu.make_async_copy(
                    src.at[rr, :], w_all.at[d, rr, pl.ds(lo, n)], loc_sem.at[p, c, i]
                )
                cp.start()
                trio.append(cp)
            own.append((p, c, trio))

    barrier = pltpu.get_barrier_semaphore()

    @pl.loop(1, everyone)
    def _(i):
        other = (me + i) % everyone
        pl.semaphore_signal(
            barrier, inc=1, device_id=(other // M, other % M), device_id_type=MESH
        )

    xown = pltpu.make_async_copy(tok_ref, x_all.at[m], one_sem.at[0])
    early = [
        pltpu.make_async_copy(cos_hbm, cos_ref, one_sem.at[1]),
        pltpu.make_async_copy(sin_hbm, sin_ref, one_sem.at[2]),
        pltpu.make_async_copy(wout_hbm, wout_ref, one_sem.at[3]),
    ]
    for b in range(S):
        early.append(pltpu.make_async_copy(
            tok_ref.at[pl.ds((b + 1) * L - 16, 16), :], tail_tok.at[b], one_sem.at[4 + b]
        ))
    pl.semaphore_wait(barrier, everyone - 1)

    pending = []

    def remote(src, dst, ss, rs, to, cond=None):
        cp = pltpu.make_async_remote_copy(
            src_ref=src, dst_ref=dst, send_sem=ss, recv_sem=rs, device_id=to, device_id_type=MESH
        )
        if cond is None:
            cp.start()
        else:
            pl.when(cond)(cp.start)
        pending.append((cp, cond))

    def local(src, dst, rs, cond=None):
        cp = pltpu.make_async_copy(src, dst, rs)
        if cond is None:
            cp.start()
        else:
            pl.when(cond)(cp.start)

    def arrive(buf, sem, n):
        for i in range(n):
            pltpu.make_async_copy(buf.at[i], buf.at[i], sem.at[i]).wait()

    def xsend(hop, c, side):
        rr = pl.ds(c * xpiece, xpiece)
        owner = m - hop if side == 0 else m + hop
        to = m + 1 if side == 0 else m - 1
        return pltpu.make_async_remote_copy(
            src_ref=(tok_ref.at[rr, :] if hop == 0 else x_all.at[owner, rr, :]),
            dst_ref=x_all.at[owner, rr, :],
            send_sem=xs_sem.at[hop, c, side],
            recv_sem=xr_sem.at[hop, c, side],
            device_id=(d, to),
            device_id_type=MESH,
        )

    def xpred(hop, side):
        if side == 0:
            return (m < M - 1) & (m - hop >= 0)
        return (m > 0) & (m + hop < M)

    def xstart(hop, c):
        for side in range(2):
            @pl.when(xpred(hop, side))
            def _(side=side):
                xsend(hop, c, side).start()

    def xwait(hop, c):
        rr = pl.ds(c * xpiece, xpiece)
        for side in range(2):
            owner = m - hop - 1 if side == 0 else m + hop + 1
            ok = (m - hop - 1 >= 0) if side == 0 else (m + hop + 1 < M)

            @pl.when(ok)
            def _(side=side, owner=owner):
                pltpu.make_async_copy(
                    x_all.at[owner, rr, :], x_all.at[owner, rr, :], xr_sem.at[hop, c, side]
                ).wait()

    def wcopy(mask, p, c, bit, send_sem, recv_sem):
        owner = flip(d, mask)
        rr = wrows(p, c)
        remote(w_all.at[owner, rr, :], w_all.at[owner, rr, :], send_sem, recv_sem,
               (flip(d, bit), m))

    def wsend(mask, p, c, step):
        bit = plan[p][0][step]
        wcopy(mask, p, c, bit, ps_sem.at[p, mask // 2, c, step],
              pr_sem.at[p, (mask ^ bit) // 2, c])

    def csend(mask, p, c):
        wcopy(mask, p, c, 1, cs_sem.at[p, mask // 2, c], cr_sem.at[p, mask // 2, c])

    def wwait(mask, p, c, sem):
        owner = flip(d, mask)
        rr = wrows(p, c)
        pltpu.make_async_copy(w_all.at[owner, rr, :], w_all.at[owner, rr, :], sem).wait()

    steps = len(plan[0][0])
    for i, (p, c, trio) in enumerate(own):
        for cp in trio:
            cp.wait()
        wsend(0, p, c, 0)
        if i == parts - 1:
            for cc in range(xchunks):
                xstart(0, cc)
    for step in range(1, steps):
        for c in range(chunks):
            for p in range(parts):
                wsend(0, p, c, step)
    for c in range(chunks):
        for p in range(parts):
            csend(0, p, c)
    xown.start()
    for cp in early:
        cp.start()
    for i in range(1, D):
        to = (d + i) % D
        remote(contrib_ref.at[to], dir_all.at[d], s2.at[i], r2.at[d], (to, m))
    local(contrib_ref.at[d], dir_all.at[d], r2.at[d])

    rounds = len(plan[0][1])
    wevents = [(r, c) for r in range(rounds) for c in range(chunks)]
    xevents = [(h, c) for h in range(M - 1) for c in range(xchunks)]
    merged = sorted(
        [((i + 1) / len(wevents), 1, e) for i, e in enumerate(wevents)]
        + [(0.8 * (i + 1) / len(xevents), 0, e) for i, e in enumerate(xevents)]
    )

    def use(owner, lo, n):
        base = owner * depth
        shard = base // width
        col = pl.multiple_of(base % width + lo, 128 if n % 128 == 0 else n)
        acc[...] += jnp.dot(
            x_all[shard, :, pl.ds(col, n)], w_all[owner, pl.ds(lo, n), :],
            preferred_element_type=F32,
        )

    every_piece = {(p, c) for p in range(parts) for c in range(chunks)}
    got = {0: set(every_piece)}
    used = set()
    late = []

    def sweep():
        whole = [k for k in got if got[k] == every_piece and not any((k, q) in used for q in every_piece)]
        for mask in whole:
            use(flip(d, mask), 0, depth)
        for mask in whole:
            for p, c in sorted(every_piece):
                wwait(mask + 1, p, c, cr_sem.at[p, mask // 2, c])
                used.add((mask, (p, c)))
            use(flip(d, mask + 1), 0, depth)
        fresh = sorted((k, q) for k in got for q in got[k] if (k, q) not in used)
        if piece % 128:
            fresh = []
        for mask, (p, c) in fresh:
            used.add((mask, (p, c)))
            use(flip(d, mask), (p * chunks + c) * piece, piece)
        finish()
        late.extend(fresh)

    def finish():
        for mask, (p, c) in late:
            wwait(mask + 1, p, c, cr_sem.at[p, mask // 2, c])
            use(flip(d, mask + 1), (p * chunks + c) * piece, piece)
        late.clear()

    x_left = len(xevents)
    for _, kind, (a, c) in merged:
        if kind == 0:
            xwait(a, c)
            if a + 1 < M - 1:
                xstart(a + 1, c)
            x_left -= 1
            if x_left == 0:
                xown.wait()
                total = jnp.zeros((rows, 1), F32)
                for k in range(M):
                    xv = x_all[k].astype(F32)
                    total = total + jnp.sum(xv * xv, axis=1, keepdims=True)
                inv = lax.rsqrt(total / model_width + 1e-05)
                for h in range(M - 1):
                    for cc in range(xchunks):
                        for side in range(2):
                            @pl.when(xpred(h, side))
                            def _(h=h, cc=cc, side=side):
                                xsend(h, cc, side).wait_send()
                for k in range(M):
                    g = gain_ref[:, k * width:(k + 1) * width].astype(F32)
                    x_all[k] = (x_all[k].astype(F32) * inv * g).astype(BF16)
                acc[...] = jnp.zeros_like(acc)
                sweep()
        else:
            for p in range(parts):
                mask, step = plan[p][1][a]
                wwait(mask, p, c, pr_sem.at[p, mask // 2, c])
                for later in range(step + 1, steps):
                    wsend(mask, p, c, later)
                csend(mask, p, c)
                got.setdefault(mask, set()).add((p, c))
            if x_left == 0:
                sweep()
    finish()

    for cp in early:
        cp.wait()
    half = HEAD_SIZE // 2

    def rope(x, cos, sin):
        turned = jnp.concatenate([x[:, half:], x[:, :half]], axis=1)
        return (x * cos + turned * sin).astype(BF16)

    def softmax(logits):
        e = jnp.exp(logits - jnp.max(logits, axis=1, keepdims=True))
        return (e / jnp.sum(e, axis=1, keepdims=True)).astype(BF16)

    def scaled(q, k):
        return lax.dot_general(
            q, k, (((1,), (1,)), ((), ())), preferred_element_type=F32
        ) / math.sqrt(HEAD_SIZE)

    for b in range(S):
        span_b = slice(b * L, (b + 1) * L)
        at_last = (b + 1) * L - 1
        for n in range(kv_heads):
            lo = qw + n * HEAD_SIZE
            k = rope(acc[span_b, lo:lo + HEAD_SIZE], cos_ref[...], sin_ref[...])
            v = acc[span_b, lo + kw:lo + kw + HEAD_SIZE].astype(BF16)
            k_s[b * kv_heads + n] = k
            v_s[b * kv_heads + n] = v
            for g in range(G):
                h = n * G + g
                q_s[g:g + 1, :] = acc[at_last:at_last + 1, h * HEAD_SIZE:(h + 1) * HEAD_SIZE]
            q = rope(q_s[...], cos_ref[L - 1:L, :], sin_ref[L - 1:L, :])
            mixed = jnp.dot(softmax(scaled(q, k)), v, preferred_element_type=F32)
            mixed = mixed.astype(BF16).astype(F32)
            for g in range(G):
                h = n * G + g
                last_src[b:b + 1, h * HEAD_SIZE:(h + 1) * HEAD_SIZE] = mixed[g:g + 1, :]
    for i in range(1, D):
        to = (d + i) % D
        remote(last_src, last_all.at[d], s1.at[i], r1.at[d], (to, m))
    local(last_src, last_all.at[d], r1.at[d])

    ahead = lax.broadcasted_iota(jnp.int32, (L, L), 0) >= lax.broadcasted_iota(jnp.int32, (L, L), 1)

    def attend(first, end):
        for b in range(S):
            @pl.loop(first, end)
            def _(h):
                at = pl.ds(pl.multiple_of(h * HEAD_SIZE, HEAD_SIZE), HEAD_SIZE)
                n = b * kv_heads + h // G
                q = rope(acc[pl.ds(b * L, L), at], cos_ref[...], sin_ref[...])
                logits = jnp.where(ahead, scaled(q, k_s[n]), -1e30)
                mixed = jnp.dot(softmax(logits), v_s[n], preferred_element_type=F32).astype(BF16)
                head_ref[pl.ds(b * L, L), at] = mixed
                column = jnp.sum(mixed.astype(F32), axis=0, keepdims=True)
                if b == 0:
                    tot_src[:, at] = column
                else:
                    tot_src[:, at] += column

    cut = heads * 3 // 8
    attend(0, cut)
    arrive(last_all, r1, D)
    for j in range(D):
        rows_a[j * S:(j + 1) * S, 0:qw] = last_all[j]
    w = wout_ref[...]
    partial = jnp.dot(rows_a[:, 0:qw].astype(BF16), w, preferred_element_type=F32)
    for j in range(D):
        out_src[j] = partial[j * S:(j + 1) * S, :]
    span = d // R
    slot = (d % R) * M + m
    for i in range(D):
        to = (d + i) % D
        if i == 0:
            remote(out_src.at[to], out_all.at[slot], s3.at[i], r3.at[slot], (to, span), m != span)
            local(out_src.at[to], out_all.at[slot], r3.at[slot], m == span)
        else:
            remote(out_src.at[to], out_all.at[slot], s3.at[i], r3.at[slot], (to, span))

    attend(cut, heads)
    for i in range(1, D):
        to = (d + i) % D
        remote(tot_src, tot_all.at[d], s4.at[i], r4.at[d], (to, m))
    local(tot_src, tot_all.at[d], r4.at[d])
    arrive(dir_all, r2, D)
    direction = dir_all[0]
    for j in range(1, D):
        direction = direction + dir_all[j]
    weighted = fgain_ref[...].astype(F32) * direction

    arrive(out_all, r3, D)
    pieces = []
    for jj in range(R):
        part_sum = out_all[jj * M]
        for k in range(1, M):
            part_sum = part_sum + out_all[jj * M + k]
        pieces.append(part_sum)
    attn_last = jnp.concatenate(pieces, axis=1).astype(BF16).astype(F32)
    toks = [tail_tok[b].astype(F32)[15:16, :] for b in range(S)]
    residual = (toks[0] if S == 1 else jnp.concatenate(toks, axis=0)) + attn_last
    sq_src[0] = jnp.broadcast_to(jnp.sum(residual * residual, axis=1, keepdims=True), (S, 128))
    sq_src[1] = jnp.broadcast_to(jnp.sum(residual * weighted, axis=1, keepdims=True), (S, 128))
    for i in range(1, M):
        to = (m + i) % M
        remote(sq_src, sq_all.at[m], s5.at[i], r5.at[m], (d, to))
    local(sq_src, sq_all.at[m], r5.at[m])
    arrive(sq_all, r5, M)
    square = sq_all[0, 0]
    product = sq_all[0, 1]
    for k in range(1, M):
        square = square + sq_all[k, 0]
        product = product + sq_all[k, 1]
    inverse = lax.rsqrt(square / model_width + 1e-05)
    metric = inverse * product
    metric_ref[...] = metric[:, 0:1]
    grad = weighted * inverse[:, 0:1] - residual * (
        metric * inverse * inverse / model_width
    )[:, 0:1]
    for jj in range(R):
        g_src[jj] = grad[:, jj * cols:(jj + 1) * cols].astype(BF16).astype(F32)
    for i in range(M - 1, -1, -1):
        k = (m + i) % M
        for jj in range(R):
            to = m * R + jj
            if i == 0:
                remote(g_src.at[jj], g_all.at[d], s6.at[jj, i], r6.at[d], (to, k), to != d)
                local(g_src.at[jj], g_all.at[d], r6.at[d], to == d)
            else:
                remote(g_src.at[jj], g_all.at[d], s6.at[jj, i], r6.at[d], (to, k))
    arrive(tot_all, r4, D)
    mean = tot_all[0]
    for j in range(1, D):
        mean = mean + tot_all[j]
    mean = mean / token_count
    arrive(g_all, r6, D)
    for j in range(D):
        rows_a[j * S:(j + 1) * S, 0:cols] = g_all[j]
    hg = lax.dot_general(
        rows_a[:, 0:cols].astype(BF16), w, (((1,), (1,)), ((), ())), preferred_element_type=F32
    )
    for j in range(D):
        hg_src[j] = hg[j * S:(j + 1) * S, :]
    for i in range(1, D):
        to = (d + i) % D
        remote(hg_src.at[to], hg_all.at[d], s7.at[i], r7.at[d], (to, m))
    local(hg_src.at[d], hg_all.at[d], r7.at[d])
    arrive(hg_all, r7, D)
    grads = hg_all[0]
    for j in range(1, D):
        grads = grads + hg_all[j]
    gap = (mean - last_src[...]) * grads
    lane = lax.broadcasted_iota(jnp.int32, (S, heads), 1)
    scores = jnp.zeros((S, heads), F32)
    for h in range(heads):
        part = jnp.sum(gap[:, h * HEAD_SIZE:(h + 1) * HEAD_SIZE], axis=1, keepdims=True)
        scores = jnp.where(lane == h, part, scores)
    scores_ref[...] = scores
    for cp, cond in pending:
        if cond is None:
            cp.wait_send()
        else:
            pl.when(cond)(cp.wait_send)


def tables():
    half = HEAD_SIZE // 2
    inv_freq = np.exp(np.arange(half) * (-2.0 * math.log(500000.0) / HEAD_SIZE))
    angles = np.arange(SEQUENCE_LENGTH)[:, None] * inv_freq[None, :]
    c, s = np.cos(angles), np.sin(angles)
    cos = np.concatenate([c, c], axis=1).astype(np.float32)
    return cos, np.concatenate([-s, s], axis=1).astype(np.float32)


def whole(D, M, tokens, gain, wq, wk, wv, w_out, contrib, final_gain):
    rows, width = tokens.shape
    S = rows // SEQUENCE_LENGTH
    depth = wq.shape[0]
    entries, cols = w_out.shape
    total = wq.shape[1] + wk.shape[1] + wv.shape[1]
    heads, kv_heads = wq.shape[1] // HEAD_SIZE, wk.shape[1] // HEAD_SIZE
    parts = len(spread_plan(D))
    steps = len(spread_plan(D)[0][0])
    chunks = max(1, min(4, depth // (128 * parts)))
    xchunks = 2
    half = D // 2
    R = D // M
    cos, sin = tables()
    DMA = pltpu.SemaphoreType.DMA
    ANY = pl.BlockSpec(memory_space=pl.ANY)
    V = pl.BlockSpec(memory_space=pltpu.VMEM)

    def f(*shape):
        return pltpu.VMEM(shape, F32)

    def h(*shape):
        return pltpu.VMEM(shape, BF16)

    return pl.pallas_call(
        functools.partial(whole_kernel, D, M, chunks, xchunks, rows * D),
        name="whole",
        out_shape=[
            jax.ShapeDtypeStruct((rows, entries), BF16),
            jax.ShapeDtypeStruct((S, heads), F32),
            jax.ShapeDtypeStruct((S, 1), F32),
        ],
        in_specs=[ANY, V, ANY, ANY, ANY, ANY, ANY, ANY, ANY, V],
        out_specs=[V, V, V],
        scratch_shapes=[
            h(M, rows, width), h(D, depth, total), f(rows, total),
            f(SEQUENCE_LENGTH, HEAD_SIZE), f(SEQUENCE_LENGTH, HEAD_SIZE),
            h(entries, cols), h(S, 16, width), f(heads // kv_heads, HEAD_SIZE),
            h(S * kv_heads, SEQUENCE_LENGTH, HEAD_SIZE), h(S * kv_heads, SEQUENCE_LENGTH, HEAD_SIZE),
            f(1, entries), f(S, entries), f(D, 1, entries), f(D, S, entries),
            f(D * S, max(entries, cols)), f(D, S, cols), f(D, S, cols), f(D, S, width),
            f(2, S, 128), f(M, 2, S, 128), f(R, S, cols), f(D, S, cols),
            f(D, S, entries), f(D, S, entries),
            DMA((parts, chunks, 3)), DMA((4 + S,)),
            DMA((M - 1, xchunks, 2)), DMA((M - 1, xchunks, 2)),
            DMA((parts, half, chunks, steps)), DMA((parts, half, chunks)),
            DMA((parts, half, chunks)), DMA((parts, half, chunks)),
            DMA((D,)), DMA((D,)), DMA((D,)), DMA((D,)), DMA((D,)), DMA((D,)), DMA((D,)), DMA((D,)),
            DMA((M,)), DMA((M,)), DMA((R, M)), DMA((D,)), DMA((D,)), DMA((D,)),
        ],
        compiler_params=pltpu.CompilerParams(
            collective_id=0, has_side_effects=True, vmem_limit_bytes=56 * 1024 * 1024
        ),
    )(tokens, gain, wq, wk, wv, jnp.asarray(cos), jnp.asarray(sin), w_out, contrib,
      final_gain.reshape(1, width))


GROUP = 16


def pick_kernel(per, at_ref, *refs):
    blocks, out_ref = refs[:-1], refs[-1]
    step = pl.program_id(0)
    total = pl.num_programs(0) * per
    where = lax.broadcasted_iota(jnp.int32, (GROUP, 1), 0)
    for i in range(per):
        rows = []
        for side in range(2):
            at = at_ref[side * total + step * per + i]
            block = blocks[side * per + i][...].astype(F32)
            hit = (where == at % GROUP) & (at >= 0)
            rows.append(jnp.sum(jnp.where(hit, block, 0.0), axis=0, keepdims=True))
        out_ref[i] = rows[0] - rows[1]


def pick(unembed, at):
    width = unembed.shape[1]
    n = at.shape[0] // 2
    per = min(8, n)

    def spec(side, i):
        def index(step, at_ref):
            return jnp.maximum(at_ref[side * n + step * per + i], 0) // GROUP, 0
        return pl.BlockSpec((GROUP, width), index)

    return pl.pallas_call(
        functools.partial(pick_kernel, per),
        name="pick",
        grid_spec=pltpu.PrefetchScalarGridSpec(
            num_scalar_prefetch=1,
            grid=(n // per,),
            in_specs=[spec(side, i) for side in range(2) for i in range(per)],
            out_specs=pl.BlockSpec((per, 1, width), lambda step, at_ref: (step, 0, 0)),
        ),
        out_shape=jax.ShapeDtypeStruct((n, 1, width), F32),
    )(at, *([unembed] * (2 * per)))


def per_device(
    D, M, tokens, attn_gain, w_query, key_w, value_w, w_out, final_gain, unembed,
    clean_ids, corrupt_ids,
):
    S = tokens.shape[0] // SEQUENCE_LENGTH
    vocab_rows, width = unembed.shape
    at = jnp.concatenate([clean_ids, corrupt_ids]) - lax.axis_index("dp") * vocab_rows
    at = jnp.where(at < vocab_rows, jnp.maximum(at, -1), -1)
    contrib = pick(unembed, at).reshape(D, S, width)
    head_out, scores, metric = whole(
        D, M, tokens, attn_gain.reshape(1, -1), w_query, key_w, value_w, w_out, contrib, final_gain
    )
    return head_out, scores, metric.reshape(S)


def solution(mesh):
    in_specs = (
        P("dp", "mp"), P(), P("dp", "mp"), P("dp", "mp"), P("dp", "mp"),
        P("mp", "dp"), P("mp"), P("dp", "mp"), P(), P(),
    )
    out_specs = (P("dp", "mp"), P("dp", "mp"), P("dp"))
    return jax.shard_map(
        functools.partial(per_device, mesh.shape["dp"], mesh.shape["mp"]),
        mesh=mesh, in_specs=in_specs, out_specs=out_specs, check_vma=False,
    )
```

time: 147 us -> 133 us (0.905)
  Pallas kernels: 132 us -> 123 us
  local copies, waits for them, and re-layouts: 8.73 us -> 5.61 us
    pallas_call x3 -> x2, Pallas kernels: 132 us -> 123 us  [the longest x1 120 us: whole(): pl.pallas_call(functools.partial(whole_kernel, D, M, chunks, xchunks, row...]
    gather x2 -> x0, local copies, waits for them, and re-layouts: 3.07 us -> none  [picked(): rows = jnp.take(unembed, jnp.clip(at, 0, vocab_rows - 1), axis=0)]
    unnamed x5 -> x2, local copies, waits for them, and re-layouts: 2.8 us -> 2.97 us
where the time goes in v2:
time: 133 us
  Pallas kernels  123 us (92%)
  local copies, waits for them, and re-layouts  5.61 us (4%)
  between operations  2.45 us (2%)
    pallas_call x1, Pallas kernels, whole(): pl.pallas_call(functools.partial(whole_kernel, D, M, chunks, xchunks, row...  120 us
    pallas_call x1, Pallas kernels, pick(): pl.pallas_call(functools.partial(pick_kernel, per), name='pick', grid_spe...  3.44 us
    unnamed x2, local copies, waits for them, and re-layouts  2.97 us

profile of v2, /device:TPU:0, one launch (start us, length us, event | category | flops | bytes accessed | tf_op | source)
XLA Modules:
  0.0 132.7 jit_solution(3694968764117784600)
XLA Ops:
  0.6 1.3 compare_select_fusion.at_ref
  1.9 1.3 reshape.16.fgain_ref
  3.2 1.3 %reshape.15.gain_ref = bf16[1,8192]{1,0:T(2,128)(2,1)} reshape(bf16[8192]{0:T(1024)(128)(2,1)} %param.13) | data formatting | bytes 32768 | tf_op jit(solution)/shard_map/reshape | solution.py:580
  4.5 3.4 %pick.1.contrib_ref = f32[8,1,2048]{2,1,0:T(1,128)} custom-call(s32[16]{0:T(128)} %compare_select_fusion.at_ref, bf16[8016,2048]{1,0:T(8,128)(2,1)} %refs_15_.1, bf16[8016,2048]{1,0:T(8,128)(2,1)} %refs_15_.1, bf16[8016,2048]{1,0:T(8,128)(2,1)} %refs_15_.1, bf16[8016,2048]{1,0:T(8,128)(2,1)} %refs_15_.1, bf16[8016,2048]{1,0:T(8,128)(2,1)} %refs_15_.1, ...), custom_call_target="tpu_custom_call" | custom-call | tf_op jit(solution)/shard_map/pick/pallas_call | solution.py:557
  8.0 120.0 %whole.1 = (bf16[256,1024]{1,0:T(8,128)(2,1)}, f32[1,8]{1,0:T(1,128)}, f32[1,1]{1,0:T(1,128)}) custom-call(bf16[256,2048]{1,0:T(8,128)(2,1)} %tok_ref.1, bf16[1,8192]{1,0:T(2,128)(2,1)} %reshape.15.gain_ref, bf16[1024,1024]{1,0:T(8,128)(2,1)} %wq_ref.1, bf16[1024,128]{1,0:T(8,128)(2,1)} %wk_ref.1, bf16[1024,128]{1,0:T(8,128)(2,1)} %wv_ref.1, ...), custom_call_target="tpu_custom_call" | custom-call | tf_op jit(solution)/shard_map/whole/pallas_call | solution.py:496
  127.9 1.9 %copy.18 = bf16[256,1024]{1,0:T(8,128)(2,1)} copy(bf16[256,1024]{1,0:T(8,128)(2,1)} %get-tuple-element.12) | data formatting | bytes 1048576
  129.8 1.1 copy.19

commit v3 on v2

--- a/solution.py
+++ b/solution.py
@@ -52,7 +52,7 @@
     head_ref, scores_ref, metric_ref,
     x_all, w_all, acc, cos_ref, sin_ref, wout_ref, tail_tok, q_s, k_s, v_s, tot_src,
     last_src, tot_all, last_all, rows_a, out_src, out_all, dir_all, sq_src, sq_all,
-    g_src, g_all, hg_src, hg_all,
+    g_src, g_all, hg_src, hg_all, rows_g,
     loc_sem, one_sem, xs_sem, xr_sem, ps_sem, pr_sem, cs_sem, cr_sem,
     s1, r1, s2, r2, s3, r3, s4, r4, s5, r5, s6, r6, s7, r7,
 ):
@@ -236,16 +236,14 @@
     got = {0: set(every_piece)}
     used = set()
     late = []
-
-    def sweep():
+    todo = []
+
+    def sweep(left):
         whole = [k for k in got if got[k] == every_piece and not any((k, q) in used for q in every_piece)]
         for mask in whole:
-            use(flip(d, mask), 0, depth)
-        for mask in whole:
-            for p, c in sorted(every_piece):
-                wwait(mask + 1, p, c, cr_sem.at[p, mask // 2, c])
-                used.add((mask, (p, c)))
-            use(flip(d, mask + 1), 0, depth)
+            todo.append((mask, False))
+            used.update((mask, q) for q in every_piece)
+        todo.extend((mask, True) for mask in whole)
         fresh = sorted((k, q) for k in got for q in got[k] if (k, q) not in used)
         if piece % 128:
             fresh = []
@@ -254,6 +252,15 @@
             use(flip(d, mask), (p * chunks + c) * piece, piece)
         finish()
         late.extend(fresh)
+        drain(-(-len(todo) // max(1, left - 1)))
+
+    def drain(n):
+        for mask, paired in todo[:n]:
+            if paired:
+                for p, c in sorted(every_piece):
+                    wwait(mask + 1, p, c, cr_sem.at[p, mask // 2, c])
+            use(flip(d, mask + int(paired)), 0, depth)
+        del todo[:n]
 
     def finish():
         for mask, (p, c) in late:
@@ -282,10 +289,9 @@
                             def _(h=h, cc=cc, side=side):
                                 xsend(h, cc, side).wait_send()
                 for k in range(M):
-                    g = gain_ref[:, k * width:(k + 1) * width].astype(F32)
+                    g = gain_ref[k * width:(k + 1) * width].astype(F32).reshape(1, width)
                     x_all[k] = (x_all[k].astype(F32) * inv * g).astype(BF16)
                 acc[...] = jnp.zeros_like(acc)
-                sweep()
         else:
             for p in range(parts):
                 mask, step = plan[p][1][a]
@@ -295,7 +301,8 @@
                 csend(mask, p, c)
                 got.setdefault(mask, set()).add((p, c))
             if x_left == 0:
-                sweep()
+                sweep(len(wevents) - wevents.index((a, c)))
+    drain(len(todo))
     finish()
 
     for cp in early:
@@ -384,7 +391,7 @@
     direction = dir_all[0]
     for j in range(1, D):
         direction = direction + dir_all[j]
-    weighted = fgain_ref[...].astype(F32) * direction
+    weighted = fgain_ref[...].astype(F32).reshape(1, width) * direction
 
     arrive(out_all, r3, D)
     pieces = []
@@ -402,6 +409,18 @@
         to = (m + i) % M
         remote(sq_src, sq_all.at[m], s5.at[i], r5.at[m], (d, to))
     local(sq_src, sq_all.at[m], r5.at[m])
+    for jj in range(R):
+        g_src[jj, 0:S, :] = weighted[:, jj * cols:(jj + 1) * cols]
+        g_src[jj, S:2 * S, :] = residual[:, jj * cols:(jj + 1) * cols]
+    for i in range(M - 1, -1, -1):
+        k = (m + i) % M
+        for jj in range(R):
+            to = m * R + jj
+            if i == 0:
+                remote(g_src.at[jj], g_all.at[d], s6.at[jj, i], r6.at[d], (to, k), to != d)
+                local(g_src.at[jj], g_all.at[d], r6.at[d], to == d)
+            else:
+                remote(g_src.at[jj], g_all.at[d], s6.at[jj, i], r6.at[d], (to, k))
     arrive(sq_all, r5, M)
     square = sq_all[0, 0]
     product = sq_all[0, 1]
@@ -411,20 +430,7 @@
     inverse = lax.rsqrt(square / model_width + 1e-05)
     metric = inverse * product
     metric_ref[...] = metric[:, 0:1]
-    grad = weighted * inverse[:, 0:1] - residual * (
-        metric * inverse * inverse / model_width
-    )[:, 0:1]
-    for jj in range(R):
-        g_src[jj] = grad[:, jj * cols:(jj + 1) * cols].astype(BF16).astype(F32)
-    for i in range(M - 1, -1, -1):
-        k = (m + i) % M
-        for jj in range(R):
-            to = m * R + jj
-            if i == 0:
-                remote(g_src.at[jj], g_all.at[d], s6.at[jj, i], r6.at[d], (to, k), to != d)
-                local(g_src.at[jj], g_all.at[d], r6.at[d], to == d)
-            else:
-                remote(g_src.at[jj], g_all.at[d], s6.at[jj, i], r6.at[d], (to, k))
+    fall = (metric * inverse * inverse / model_width)[:, 0:1]
     arrive(tot_all, r4, D)
     mean = tot_all[0]
     for j in range(1, D):
@@ -432,20 +438,26 @@
     mean = mean / token_count
     arrive(g_all, r6, D)
     for j in range(D):
-        rows_a[j * S:(j + 1) * S, 0:cols] = g_all[j]
-    hg = lax.dot_general(
-        rows_a[:, 0:cols].astype(BF16), w, (((1,), (1,)), ((), ())), preferred_element_type=F32
+        rows_g[2 * j * S:2 * (j + 1) * S, :] = g_all[j]
+    exact = rows_g[...]
+    coarse = exact.astype(BF16)
+    fine = (exact - coarse.astype(F32)).astype(BF16)
+    both = lax.dot_general(
+        jnp.concatenate([coarse, fine], axis=0), w, (((1,), (1,)), ((), ())),
+        preferred_element_type=F32,
     )
+    hg = both[:2 * D * S] + both[2 * D * S:]
     for j in range(D):
-        hg_src[j] = hg[j * S:(j + 1) * S, :]
+        hg_src[j] = hg[2 * j * S:2 * (j + 1) * S, :]
     for i in range(1, D):
         to = (d + i) % D
         remote(hg_src.at[to], hg_all.at[d], s7.at[i], r7.at[d], (to, m))
     local(hg_src.at[d], hg_all.at[d], r7.at[d])
     arrive(hg_all, r7, D)
-    grads = hg_all[0]
+    joint = hg_all[0]
     for j in range(1, D):
-        grads = grads + hg_all[j]
+        joint = joint + hg_all[j]
+    grads = joint[0:S] * inverse[:, 0:1] - joint[S:2 * S] * fall
     gap = (mean - last_src[...]) * grads
     lane = lax.broadcasted_iota(jnp.int32, (S, heads), 1)
     scores = jnp.zeros((S, heads), F32)
@@ -510,8 +522,8 @@
             h(S * kv_heads, SEQUENCE_LENGTH, HEAD_SIZE), h(S * kv_heads, SEQUENCE_LENGTH, HEAD_SIZE),
             f(1, entries), f(S, entries), f(D, 1, entries), f(D, S, entries),
             f(D * S, max(entries, cols)), f(D, S, cols), f(D, S, cols), f(D, S, width),
-            f(2, S, 128), f(M, 2, S, 128), f(R, S, cols), f(D, S, cols),
-            f(D, S, entries), f(D, S, entries),
+            f(2, S, 128), f(M, 2, S, 128), f(R, 2 * S, cols), f(D, 2 * S, cols),
+            f(D, 2 * S, entries), f(D, 2 * S, entries), f(2 * D * S, cols),
             DMA((parts, chunks, 3)), DMA((4 + S,)),
             DMA((M - 1, xchunks, 2)), DMA((M - 1, xchunks, 2)),
             DMA((parts, half, chunks, steps)), DMA((parts, half, chunks)),
@@ -523,48 +535,49 @@
             collective_id=0, has_side_effects=True, vmem_limit_bytes=56 * 1024 * 1024
         ),
     )(tokens, gain, wq, wk, wv, jnp.asarray(cos), jnp.asarray(sin), w_out, contrib,
-      final_gain.reshape(1, width))
+      final_gain)
 
 
 GROUP = 16
 
 
-def pick_kernel(per, at_ref, *refs):
+def pick_kernel(per, vocab_rows, clean_ref, corrupt_ref, *refs):
     blocks, out_ref = refs[:-1], refs[-1]
     step = pl.program_id(0)
-    total = pl.num_programs(0) * per
+    start = lax.axis_index("dp") * vocab_rows
     where = lax.broadcasted_iota(jnp.int32, (GROUP, 1), 0)
     for i in range(per):
         rows = []
         for side in range(2):
-            at = at_ref[side * total + step * per + i]
+            at = (clean_ref, corrupt_ref)[side][step * per + i] - start
             block = blocks[side * per + i][...].astype(F32)
-            hit = (where == at % GROUP) & (at >= 0)
+            hit = (where == at % GROUP) & (at >= 0) & (at < vocab_rows)
             rows.append(jnp.sum(jnp.where(hit, block, 0.0), axis=0, keepdims=True))
         out_ref[i] = rows[0] - rows[1]
 
 
-def pick(unembed, at):
-    width = unembed.shape[1]
-    n = at.shape[0] // 2
+def pick(unembed, clean_ids, corrupt_ids):
+    vocab_rows, width = unembed.shape
+    n = clean_ids.shape[0]
     per = min(8, n)
 
     def spec(side, i):
-        def index(step, at_ref):
-            return jnp.maximum(at_ref[side * n + step * per + i], 0) // GROUP, 0
+        def index(step, *ids):
+            at = ids[side][step * per + i] - lax.axis_index("dp") * vocab_rows
+            return jnp.clip(at, 0, vocab_rows - 1) // GROUP, 0
         return pl.BlockSpec((GROUP, width), index)
 
     return pl.pallas_call(
-        functools.partial(pick_kernel, per),
+        functools.partial(pick_kernel, per, vocab_rows),
         name="pick",
         grid_spec=pltpu.PrefetchScalarGridSpec(
-            num_scalar_prefetch=1,
+            num_scalar_prefetch=2,
             grid=(n // per,),
             in_specs=[spec(side, i) for side in range(2) for i in range(per)],
-            out_specs=pl.BlockSpec((per, 1, width), lambda step, at_ref: (step, 0, 0)),
+            out_specs=pl.BlockSpec((per, 1, width), lambda step, *ids: (step, 0, 0)),
         ),
         out_shape=jax.ShapeDtypeStruct((n, 1, width), F32),
-    )(at, *([unembed] * (2 * per)))
+    )(clean_ids, corrupt_ids, *([unembed] * (2 * per)))
 
 
 def per_device(
@@ -572,12 +585,10 @@
     clean_ids, corrupt_ids,
 ):
     S = tokens.shape[0] // SEQUENCE_LENGTH
-    vocab_rows, width = unembed.shape
-    at = jnp.concatenate([clean_ids, corrupt_ids]) - lax.axis_index("dp") * vocab_rows
-    at = jnp.where(at < vocab_rows, jnp.maximum(at, -1), -1)
-    contrib = pick(unembed, at).reshape(D, S, width)
+    width = unembed.shape[1]
+    contrib = pick(unembed, clean_ids, corrupt_ids).reshape(D, S, width)
     head_out, scores, metric = whole(
-        D, M, tokens, attn_gain.reshape(1, -1), w_query, key_w, value_w, w_out, contrib, final_gain
+        D, M, tokens, attn_gain, w_query, key_w, value_w, w_out, contrib, final_gain
     )
     return head_out, scores, metric.reshape(S)
 

time: 133 us -> 127 us (0.955)
  local copies, waits for them, and re-layouts: 5.61 us -> 2.97 us
  Pallas kernels: 123 us -> 121 us
    reshape x2 -> x0, local copies, waits for them, and re-layouts: 2.63 us -> none  [the longest x1 1.35 us: per_device(): attn_gain.reshape(1, -1)]
    pallas_call x1, Pallas kernels: 120 us -> 118 us  [whole(): pl.pallas_call(functools.partial(whole_kernel, D, M, chunks, xchunks, row...]
where the time goes in v3:
time: 127 us; the launch traced here: 126 us
  Pallas kernels  121 us (95%)
  local copies, waits for them, and re-layouts  2.97 us (2%)
  between operations  2.41 us (2%)
    pallas_call x1, Pallas kernels, whole(): pl.pallas_call(functools.partial(whole_kernel, D, M, chunks, xchunks, row...  118 us
    pallas_call x1, Pallas kernels, pick(): pl.pallas_call(functools.partial(pick_kernel, per, vocab_rows), name='pic...  3.5 us
    unnamed x2, local copies, waits for them, and re-layouts  2.97 us

profile of v3, /device:TPU:0, one launch (start us, length us, event | category | flops | bytes accessed | tf_op | source)
XLA Modules:
  0.0 126.5 jit_solution(11317653528322677618)
XLA Ops:
  0.6 3.5 %pick.1.contrib_ref = f32[8,1,2048]{2,1,0:T(1,128)} custom-call(s32[8]{0:T(128)} %clean_ref.1, s32[8]{0:T(128)} %corrupt_ref.1, bf16[8016,2048]{1,0:T(8,128)(2,1)} %refs_15_.1, bf16[8016,2048]{1,0:T(8,128)(2,1)} %refs_15_.1, bf16[8016,2048]{1,0:T(8,128)(2,1)} %refs_15_.1, bf16[8016,2048]{1,0:T(8,128)(2,1)} %refs_15_.1, bf16[8016,2048]{1,0:T(8,128)(2,1)} %refs_15_.1, ...), custom_call_target="tpu_custom_call" | custom-call | tf_op jit(solution)/shard_map/pick/pallas_call | solution.py:570
  4.1 117.6 %whole.1 = (bf16[256,1024]{1,0:T(8,128)(2,1)}, f32[1,8]{1,0:T(1,128)}, f32[1,1]{1,0:T(1,128)}) custom-call(bf16[256,2048]{1,0:T(8,128)(2,1)} %tok_ref.1, bf16[8192]{0:T(1024)(128)(2,1)} %gain_ref.1, bf16[1024,1024]{1,0:T(8,128)(2,1)} %wq_ref.1, bf16[1024,128]{1,0:T(8,128)(2,1)} %wk_ref.1, bf16[1024,128]{1,0:T(8,128)(2,1)} %wv_ref.1, ...), custom_call_target="tpu_custom_call" | custom-call | tf_op jit(solution)/shard_map/whole/pallas_call | solution.py:508
  121.7 1.9 %copy.18 = bf16[256,1024]{1,0:T(8,128)(2,1)} copy(bf16[256,1024]{1,0:T(8,128)(2,1)} %get-tuple-element.12) | data formatting | bytes 1048576
  123.6 1.1 copy.19

commit v4 on v3

--- a/solution.py
+++ b/solution.py
@@ -315,12 +315,12 @@
 
     def softmax(logits):
         e = jnp.exp(logits - jnp.max(logits, axis=1, keepdims=True))
-        return (e / jnp.sum(e, axis=1, keepdims=True)).astype(BF16)
+        return (e * (1.0 / jnp.sum(e, axis=1, keepdims=True))).astype(BF16)
 
     def scaled(q, k):
         return lax.dot_general(
             q, k, (((1,), (1,)), ((), ())), preferred_element_type=F32
-        ) / math.sqrt(HEAD_SIZE)
+        ) * (1.0 / math.sqrt(HEAD_SIZE))
 
     for b in range(S):
         span_b = slice(b * L, (b + 1) * L)

time: 127 us -> 127 us (level)
  no operation moved by 1% of the time
where the time goes in v4:
time: 127 us
  Pallas kernels  121 us (95%)
  local copies, waits for them, and re-layouts  2.97 us (2%)
  between operations  2.41 us (2%)
    pallas_call x1, Pallas kernels, whole(): pl.pallas_call(functools.partial(whole_kernel, D, M, chunks, xchunks, row...  118 us
    pallas_call x1, Pallas kernels, pick(): pl.pallas_call(functools.partial(pick_kernel, per, vocab_rows), name='pic...  3.37 us
    unnamed x2, local copies, waits for them, and re-layouts  2.97 us

profile of v4, /device:TPU:0, one launch (start us, length us, event | category | flops | bytes accessed | tf_op | source)
XLA Modules:
  0.0 126.6 jit_solution(11317653528322677618)
XLA Ops:
  0.6 3.4 %pick.1.contrib_ref = f32[8,1,2048]{2,1,0:T(1,128)} custom-call(s32[8]{0:T(128)} %clean_ref.1, s32[8]{0:T(128)} %corrupt_ref.1, bf16[8016,2048]{1,0:T(8,128)(2,1)} %refs_15_.1, bf16[8016,2048]{1,0:T(8,128)(2,1)} %refs_15_.1, bf16[8016,2048]{1,0:T(8,128)(2,1)} %refs_15_.1, bf16[8016,2048]{1,0:T(8,128)(2,1)} %refs_15_.1, bf16[8016,2048]{1,0:T(8,128)(2,1)} %refs_15_.1, ...), custom_call_target="tpu_custom_call" | custom-call | tf_op jit(solution)/shard_map/pick/pallas_call | solution.py:570
  4.0 117.8 %whole.1 = (bf16[256,1024]{1,0:T(8,128)(2,1)}, f32[1,8]{1,0:T(1,128)}, f32[1,1]{1,0:T(1,128)}) custom-call(bf16[256,2048]{1,0:T(8,128)(2,1)} %tok_ref.1, bf16[8192]{0:T(1024)(128)(2,1)} %gain_ref.1, bf16[1024,1024]{1,0:T(8,128)(2,1)} %wq_ref.1, bf16[1024,128]{1,0:T(8,128)(2,1)} %wk_ref.1, bf16[1024,128]{1,0:T(8,128)(2,1)} %wv_ref.1, ...), custom_call_target="tpu_custom_call" | custom-call | tf_op jit(solution)/shard_map/whole/pallas_call | solution.py:508
  121.8 1.9 %copy.18 = bf16[256,1024]{1,0:T(8,128)(2,1)} copy(bf16[256,1024]{1,0:T(8,128)(2,1)} %get-tuple-element.12) | data formatting | bytes 1048576
  123.7 1.1 copy.19
